TPU v7x, 256 devices: a whole 4x4x8 slice. The times are simulated.
256 devices in a mesh: frame: 16 (over z_lo, x), strip: 16 (over z_hi, y, core).
Axes of the slice: x: 4, y: 4, z: 8 (z_hi: 2, z_lo: 4; z = z_hi * 4 + z_lo), core: 2. Of those that a mesh axis runs over, the one named last changes fastest.
Arguments:
- movie: bfloat16 [128, 1024, 2048], P('frame', 'strip'), may hold values from -17 to 22, as said below
Outputs:
- lag_maps: float32 [25, 1024, 2048], P(None, 'strip', 'frame')
Inputs may be any that keep to these rules, and one draw needn't show every extreme that they name: Frames of a camera movie.
All inputs are finite; a program needn't handle non-finite values.
Results may differ from a plain program's by a relative error of at most 0.0004.
Values may be sent and summed in bfloat16 or wider, within the bound.
A program may use at most 64 MiB of HBM per device.

v0:
```python
import jax
import jax.numpy as jnp
from jax import lax
from jax.sharding import PartitionSpec as P


def padded_2(value, sides, width):
    for axis, dim in sides:
        peers, length = (lax.axis_size(axis), value.shape[dim])
        up = [(i, (i + 1) % peers) for i in range(peers - 1)]
        down = [(j, i) for i, j in up]
        last = lax.slice_in_dim(value, length - width, length, axis=dim)
        initial = lax.slice_in_dim(value, 0, width, axis=dim)
        before = lax.ppermute(last, axis, up)
        after = lax.ppermute(initial, axis, down)
        value = jnp.concatenate([before, value, after], axis=dim)
    return value


def lag_products(field, rows, columns):
    centre = field[:, 2 : 2 + rows, 2 : 2 + columns]
    products = []
    for row_lag in range(-2, 3):
        for col_lag in range(-2, 3):
            shifted = field[
                :, 2 + row_lag : 2 + row_lag + rows, 2 + col_lag : 2 + col_lag + columns
            ]
            products.append(jnp.sum(centre * shifted, axis=0))
    return jnp.stack(products)


def pad_columns(field):
    return jnp.pad(field, ((0, 0), (0, 0), (2, 2)))


def body(movie):
    frames_here, rows, width = movie.shape
    frame_count = lax.axis_size("frame")
    frames_total = frames_here * frame_count
    padded = padded_2(movie, (("strip", 1),), 2)
    raw_values = padded.astype(jnp.float32)
    pixel_mean = (
        lax.psum(jnp.sum(raw_values, axis=0).astype(jnp.bfloat16), "frame").astype(jnp.float32)
        / frames_total
    )
    fluctuation = pad_columns(raw_values - pixel_mean)
    lag_share = lax.psum_scatter(
        lag_products(fluctuation, rows, width), "frame", scatter_dimension=2, tiled=True
    )
    return lag_share / frames_total


def solution(mesh):
    return jax.shard_map(
        body,
        mesh=mesh,
        in_specs=(P("frame", "strip", None),),
        out_specs=P(None, "strip", "frame"),
        check_vma=False,
    )
```

profile of v0, /device:TPU:25, one launch (start us, length us, event | category | flops | bytes accessed | tf_op | source)
XLA Modules:
  0.0 430.5 jit_solution(7262845705202753640)
XLA Ops:
  6.5 1.3 fusion.5
  7.8 9.0 %collective-permute-start = (bf16[8,2,2048]{2,1,0:T(2,128)(2,1)S(1)}, bf16[8,2,2048]{2,1,0:T(2,128)(2,1)S(1)}, u32[]{:S(2)}, u32[]{:S(2)}) collective-permute-start(bf16[8,2,2048]{2,1,0:T(2,128)(2,1)S(1)} %get-tuple-element.36), channel_id=1, source_target_pairs={{0,1},{1,2},{2,3},{3,4},{4,5},{5,6},{6,7},{7,8},{8,9},{9,10},{10,1... | collective-permute-start | bytes 196616 | tf_op jit(solution)/shard_map/ppermute | solution.py:14
  16.9 1.9 collective-permute-start.1
  18.8 9.7 %collective-permute-done.1 = bf16[8,2,2048]{2,1,0:T(2,128)(2,1)S(1)} collective-permute-done((bf16[8,2,2048]{2,1,0:T(2,128)(2,1)S(1)}, bf16[8,2,2048]{2,1,0:T(2,128)(2,1)S(1)}, u32[]{:S(2)}, u32[]{:S(2)}) %collective-permute-start.1) | collective-permute-done | bytes 65568 | tf_op jit(solution)/shard_map/ppermute | solution.py:15
  28.5 3.1 fusion.4
  31.7 142.3 %all-reduce.3.cloned.1.call-done = bf16[68,2048]{1,0:T(8,128)(2,1)} async-done(((bf16[68,2048]{1,0:T(8,128)(2,1)}), bf16[68,2048]{1,0:T(8,128)(2,1)}) %all-reduce.3.cloned.1.call-update) | async-done | bytes 278544 | tf_op jit(solution)/shard_map/psum | solution.py:43
  174.0 1.0 convert_multiply_fusion
  175.0 0.9 convert_subtract_fusion
  175.9 2.1 copy-done
  178.0 13.1 %multiply_reduce_fusion = (f32[64,2048]{1,0:T(8,128)}, f32[64,2048]{1,0:T(8,128)}, f32[64,2048]{1,0:T(8,128)}, f32[64,2048]{1,0:T(8,128)}, f32[64,2048]{1,0:T(8,...) fusion(f32[8,68,2048]{2,1,0:T(8,128)S(1)} %convert_subtract_fusion), kind=kLoop, calls=%fused_computation.9 | loop fusion | flops 19660800 | bytes 14155776 | tf_op jit(solution)/shard_map/reduce_sum | solution.py:28
  191.0 45.1 %multiply_reduce_fusion.1 = (f32[64,2048]{1,0:T(8,128)S(1)}, f32[64,2048]{1,0:T(8,128)}, f32[64,2048]{1,0:T(8,128)}, f32[64,2048]{1,0:T(8,128)}, f32[64,2048]{1,...) fusion(f32[8,68,2048]{2,1,0:T(8,128)} %copy-done), kind=kLoop, calls=%fused_computation.10 | loop fusion | flops 29491200 | bytes 33554432 | tf_op jit(solution)/shard_map/reduce_sum | solution.py:28
  236.2 2.0 bitcast_dynamic-update-slice_fusion.24
  238.2 1.9 bitcast_dynamic-update-slice_fusion.23
  240.1 2.0 bitcast_dynamic-update-slice_fusion.22
  242.1 1.9 bitcast_dynamic-update-slice_fusion.21
  244.0 1.9 bitcast_dynamic-update-slice_fusion.20
  249.4 0.9 bitcast_dynamic-update-slice_fusion.15
  252.8 0.9 bitcast_dynamic-update-slice_fusion.11
  255.3 0.9 bitcast_dynamic-update-slice_fusion.8
  256.2 0.9 bitcast_dynamic-update-slice_fusion.7
  258.7 0.9 bitcast_dynamic-update-slice_fusion.4
  262.1 0.9 bitcast_dynamic-update-slice_fusion
  263.0 158.5 %reduce-scatter.2.cloned.1.call-done = f32[25,64,128]{2,1,0:T(8,128)} async-done(((f32[25,64,2048]{2,1,0:T(8,128)}), f32[25,64,128]{2,1,0:T(8,128)}) %reduce-scatter.2.cloned.1.call-update) | async-done | bytes 819216 | tf_op jit(solution)/shard_map/reduce_scatter | solution.py:47
  421.5 2.1 broadcast_multiply_fusion
  (50 shorter events, 11.9 us)
Async XLA Ops:
  6.5 168.4 %copy-start.1 = (bf16[8,64,2048]{2,1,0:T(8,128)(2,1)S(1)}, bf16[8,64,2048]{2,1,0:T(8,128)(2,1)}, u32[]{:S(2)}) copy-start(bf16[8,64,2048]{2,1,0:T(8,128)(2,1)} %param.1) | copy-start | bytes 6291460
  6.5 167.4 %all-reduce.3.cloned.1.call-start = ((), (), s32[]{:S(2)}) async-start(), calls=%async_computation.1 | async-start | bytes 589824 | tf_op jit(solution)/shard_map/psum | solution.py:43
  7.8 11.0 %collective-permute-start = (bf16[8,2,2048]{2,1,0:T(2,128)(2,1)S(1)}, bf16[8,2,2048]{2,1,0:T(2,128)(2,1)S(1)}, u32[]{:S(2)}, u32[]{:S(2)}) collective-permute-start(bf16[8,2,2048]{2,1,0:T(2,128)(2,1)S(1)} %get-tuple-element.36), channel_id=1, source_target_pairs={{0,1},{1,2},{2,3},{3,4},{4,5},{5,6},{6,7},{7,8},{8,9},{9,10},{10,1... | collective-permute-start | bytes 196616 | tf_op jit(solution)/shard_map/ppermute | solution.py:14
  16.9 11.6 %collective-permute-start.1 = (bf16[8,2,2048]{2,1,0:T(2,128)(2,1)S(1)}, bf16[8,2,2048]{2,1,0:T(2,128)(2,1)S(1)}, u32[]{:S(2)}, u32[]{:S(2)}) collective-permute-start(bf16[8,2,2048]{2,1,0:T(2,128)(2,1)S(1)} %get-tuple-element.37), channel_id=1, source_target_pairs={{1,0},{2,1},{3,2},{4,3},{5,4},{6,5},{7,6},{8,7},{9,8},{10,9},{11,1... | collective-permute-start | bytes 196616 | tf_op jit(solution)/shard_map/ppermute | solution.py:15
  31.6 389.9 %reduce-scatter.2.cloned.1.call-start = ((), (), s32[]{:S(2)}) async-start(), calls=%async_computation.2 | async-start | bytes 13926400 | tf_op jit(solution)/shard_map/reduce_scatter | solution.py:47
  175.9 2.1 copy-start
  236.1 9.8 %copy-start.15 = (f32[64,2048]{1,0:T(8,128)S(1)}, f32[64,2048]{1,0:T(8,128)}, u32[]{:S(2)}) copy-start(f32[64,2048]{1,0:T(8,128)} %get-tuple-element.9) | copy-start | bytes 1572868
  236.1 10.7 %copy-start.14 = (f32[64,2048]{1,0:T(8,128)S(1)}, f32[64,2048]{1,0:T(8,128)}, u32[]{:S(2)}) copy-start(f32[64,2048]{1,0:T(8,128)} %get-tuple-element.10) | copy-start | bytes 1572868
  236.2 11.5 %copy-start.8 = (f32[64,2048]{1,0:T(8,128)S(1)}, f32[64,2048]{1,0:T(8,128)}, u32[]{:S(2)}) copy-start(f32[64,2048]{1,0:T(8,128)} %get-tuple-element.32) | copy-start | bytes 1572868
  236.2 12.4 %copy-start.13 = (f32[64,2048]{1,0:T(8,128)S(1)}, f32[64,2048]{1,0:T(8,128)}, u32[]{:S(2)}) copy-start(f32[64,2048]{1,0:T(8,128)} %get-tuple-element.11) | copy-start | bytes 1572868
  236.2 13.2 %copy-start.12 = (f32[64,2048]{1,0:T(8,128)S(1)}, f32[64,2048]{1,0:T(8,128)}, u32[]{:S(2)}) copy-start(f32[64,2048]{1,0:T(8,128)} %get-tuple-element.12) | copy-start | bytes 1572868
  236.2 14.1 %copy-start.11 = (f32[64,2048]{1,0:T(8,128)S(1)}, f32[64,2048]{1,0:T(8,128)}, u32[]{:S(2)}) copy-start(f32[64,2048]{1,0:T(8,128)} %get-tuple-element.13) | copy-start | bytes 1572868
  238.2 12.9 %copy-start.7 = (f32[64,2048]{1,0:T(8,128)S(1)}, f32[64,2048]{1,0:T(8,128)}, u32[]{:S(2)}) copy-start(f32[64,2048]{1,0:T(8,128)} %get-tuple-element.16) | copy-start | bytes 1572868
  240.1 11.8 %copy-start.10 = (f32[64,2048]{1,0:T(8,128)S(1)}, f32[64,2048]{1,0:T(8,128)}, u32[]{:S(2)}) copy-start(f32[64,2048]{1,0:T(8,128)} %get-tuple-element.14) | copy-start | bytes 1572868
  242.1 10.7 %copy-start.6 = (f32[64,2048]{1,0:T(8,128)S(1)}, f32[64,2048]{1,0:T(8,128)}, u32[]{:S(2)}) copy-start(f32[64,2048]{1,0:T(8,128)} %get-tuple-element.17) | copy-start | bytes 1572868
  244.0 9.6 %copy-start.5 = (f32[64,2048]{1,0:T(8,128)S(1)}, f32[64,2048]{1,0:T(8,128)}, u32[]{:S(2)}) copy-start(f32[64,2048]{1,0:T(8,128)} %get-tuple-element.18) | copy-start | bytes 1572868
  246.0 8.5 %copy-start.4 = (f32[64,2048]{1,0:T(8,128)S(1)}, f32[64,2048]{1,0:T(8,128)}, u32[]{:S(2)}) copy-start(f32[64,2048]{1,0:T(8,128)} %get-tuple-element.19) | copy-start | bytes 1572868
  246.8 8.5 %copy-start.3 = (f32[64,2048]{1,0:T(8,128)S(1)}, f32[64,2048]{1,0:T(8,128)}, u32[]{:S(2)}) copy-start(f32[64,2048]{1,0:T(8,128)} %get-tuple-element.20) | copy-start | bytes 1572868
  247.7 8.5 %copy-start.2 = (f32[64,2048]{1,0:T(8,128)S(1)}, f32[64,2048]{1,0:T(8,128)}, u32[]{:S(2)}) copy-start(f32[64,2048]{1,0:T(8,128)} %get-tuple-element.33) | copy-start | bytes 1572868
  253.6 8.5 %copy-start.9 = (f32[64,2048]{1,0:T(8,128)S(1)}, f32[64,2048]{1,0:T(8,128)}, u32[]{:S(2)}) copy-start(f32[64,2048]{1,0:T(8,128)} %get-tuple-element.5) | copy-start | bytes 1572868
Sparse Core Ops, SparseCore 0:
  31.8 142.1 all-reduce.2
  263.1 158.3 reduce-scatter.1
where the time goes:
time: 432 us; the launch traced here: 430 us
  waiting for transfers between devices  310 us (72%)
  other arithmetic  65.3 us (15%)
  local copies, waits for them, and re-layouts  30.2 us (7%)
  between operations  13.5 us (3%)
  starting transfers between devices  11 us (3%)
    reduce_scatter x1, waiting for transfers between devices, body(): lax.psum_scatter(lag_products(fluctuation, rows, width), 'frame', scatter...  159 us
    psum x1, waiting for transfers between devices, body(): lax.psum(jnp.sum(raw_values, axis=0).astype(jnp.bfloat16), 'frame')  142 us
    reduce_sum x2, other arithmetic, lag_products(): products.append(jnp.sum(centre * shifted, axis=0))  58.2 us
    unnamed x56, local copies, waits for them, and re-layouts  28.1 us
    ppermute x1, waiting for transfers between devices, padded_2(): after = lax.ppermute(initial, axis, down)  9.66 us
    ppermute x1, starting transfers between devices, padded_2(): before = lax.ppermute(last, axis, up)  9.04 us
  transfers between devices with their start and end apart: 4, of which 3 were waited for; matrix products, arithmetic and copies ran while one was open for 0% of the time, Pallas kernels for 0%

commit v1 on v0

v1 whole, which is shorter than its diff:
```python
import functools

import jax
import jax.numpy as jnp
from jax import lax
from jax.experimental import pallas as pl
from jax.experimental.pallas import tpu as pltpu
from jax.sharding import PartitionSpec as P

MESH = pl.DeviceIdType.MESH
LANES = 128
CH = 8
REACH = 2
F32 = jnp.float32
BF16 = jnp.bfloat16


def lag_kernel(
    n_frame, n_strip, n_z, frames_total,
    movie, out, block, edges_in, edges_out, rows_in, rows_out, held, spread, picked, work,
    send_sem, recv_sem, own_sem, held_sem, edge_send, edge_recv, row_send, row_recv,
):
    frames, rows, width = movie.shape
    chunks = rows // CH
    n_x = n_frame // n_z
    me = lax.axis_index("frame")
    strip = lax.axis_index("strip")
    z, x = me // n_x, lax.rem(me, n_x)
    inverse = 1.0 / frames_total

    lane = lax.broadcasted_iota(jnp.int32, (8, LANES), 1)
    has_left, has_right = me > 0, me < n_frame - 1

    def peer(k):
        dx, dz = k // n_z, lax.rem(k, n_z)
        return lax.rem(z + dz, n_z) * n_x + lax.rem(x + dx, n_x)

    def chunk_at(step):
        return lax.rem(chunks - step, chunks)

    def columns(g):
        return pl.ds(pl.multiple_of(g * LANES, LANES), LANES)

    def block_copy(c, g, source):
        return pltpu.make_async_remote_copy(
            src_ref=movie.at[:, pl.ds(pl.multiple_of(c * CH, CH), CH), columns(g)],
            dst_ref=block.at[c, source],
            send_sem=send_sem.at[c, g], recv_sem=recv_sem.at[c, source],
            device_id={"frame": g}, device_id_type=MESH,
        )

    def own_copy(c):
        return pltpu.make_async_copy(
            movie.at[:, pl.ds(pl.multiple_of(c * CH, CH), CH), columns(me)],
            block.at[c, me], own_sem.at[c],
        )

    def edge_copy(g, source):
        return pltpu.make_async_remote_copy(
            src_ref=edges_out.at[g], dst_ref=edges_in.at[source],
            send_sem=edge_send.at[g], recv_sem=edge_recv.at[source],
            device_id={"frame": g}, device_id_type=MESH,
        )

    def row_copy(side, to):
        return pltpu.make_async_remote_copy(
            src_ref=rows_out.at[side], dst_ref=rows_in.at[side],
            send_sem=row_send.at[side], recv_sem=row_recv.at[side],
            device_id={"strip": to}, device_id_type=MESH,
        )

    above, below = jnp.maximum(strip - 1, 0), jnp.minimum(strip + 1, n_strip - 1)
    has_above, has_below = strip > 0, strip < n_strip - 1

    whole = pltpu.make_async_copy(movie, held, held_sem)
    whole.start()

    @pl.loop(0, chunks)
    def _(c):
        own_copy(c).start()

    barrier = pltpu.get_barrier_semaphore()

    @pl.loop(1, n_frame)
    def _(k):
        pl.semaphore_signal(barrier, inc=1, device_id={"frame": peer(k)}, device_id_type=MESH)

    @pl.when(has_above)
    def _():
        pl.semaphore_signal(barrier, inc=1, device_id={"strip": above}, device_id_type=MESH)

    @pl.when(has_below)
    def _():
        pl.semaphore_signal(barrier, inc=1, device_id={"strip": below}, device_id_type=MESH)

    neighbours = jnp.where(has_above, 1, 0) + jnp.where(has_below, 1, 0)
    pl.semaphore_wait(barrier, n_frame - 1 + neighbours)

    @pl.loop(0, chunks)
    def _(step):
        @pl.loop(1, n_frame)
        def _(k):
            block_copy(chunk_at(step), peer(k), me).start()

    whole.wait()
    pick_row = lax.broadcasted_iota(jnp.int32, (width, LANES), 0)
    pick_lane = lax.broadcasted_iota(jnp.int32, (width, LANES), 1)
    j = lax.rem(pick_lane, 4)
    target = (pick_lane // 4) * LANES + jnp.where(j < 2, j - 2, LANES - 2 + j)
    pick = jnp.where((pick_row == target) & (pick_lane < 4 * n_frame), 1.0, 0.0).astype(BF16)
    for f in range(frames):
        picked[pl.ds(f * rows, rows), :] = jnp.dot(held[f], pick, preferred_element_type=F32)

    @pl.loop(0, rows)
    def _(r):
        v = picked[pl.ds(r, frames, stride=rows), :]
        work[pl.ds(pl.multiple_of(r * 8, 8), 8), :] = pltpu.roll(v, 4 * lax.rem(r, 32), 1)

    group = lane // 4

    @pl.loop(0, n_frame)
    def _(g):
        for q in range(rows // 32):
            packed = jnp.zeros((8, LANES), F32)
            for r in range(32):
                v = work[pl.ds((q * 32 + r) * 8, 8), :]
                packed = jnp.where(group == lax.rem(r + g, 32), v, packed)
            edges_out[g, q] = pltpu.roll(packed, lax.rem(LANES - 4 * g, LANES), 1).astype(BF16)

    @pl.loop(1, n_frame)
    def _(k):
        edge_copy(peer(k), me).start()

    edges_in[me] = edges_out[me]

    @pl.loop(1, n_frame)
    def _(k):
        edge_copy(me, peer(k)).wait_recv()

    beside = ((lane >= LANES - 2) & has_left) | ((lane < 2) & has_right)

    def over_frames(total):
        return jnp.sum(total, axis=0, keepdims=True) * inverse

    def prepare(at, row_of, edge_of, edge_total):
        total = row_of(0)
        for i in range(1, n_frame):
            total = total + row_of(i)
        mean, edge_mean = over_frames(total), over_frames(edge_total)
        for i in range(n_frame):
            value = row_of(i) - mean
            edge = jnp.where(beside, edge_of(i) - edge_mean, 0.0)
            spread[at, i, 2] = value
            spread[at, i, 3] = pltpu.roll(jnp.where(lane < 1, edge, value), LANES - 1, 1)
            spread[at, i, 4] = pltpu.roll(jnp.where(lane < 2, edge, value), LANES - 2, 1)
            spread[at, i, 1] = pltpu.roll(jnp.where(lane >= LANES - 1, edge, value), 1, 1)
            spread[at, i, 0] = pltpu.roll(jnp.where(lane >= LANES - 2, edge, value), 2, 1)

    def work_row(i, r):
        return work[pl.ds(i * CH * 8 + r, 8, stride=CH), :]

    def edge_turn(c, r):
        return lax.rem(2 * LANES - 2 - 4 * (lax.rem(c, 32 // CH) * CH + r), LANES)

    def edge_tile(i, c):
        return edges_in[i, c // (32 // CH)].astype(F32)

    def take_chunk(c):
        @pl.loop(1, n_frame)
        def _(k):
            block_copy(c, me, peer(k)).wait_recv()

        own_copy(c).wait()
        for i in range(n_frame):
            work[pl.ds(i * CH * 8, CH * 8), :] = (
                block[c, i].astype(F32).reshape(CH * 8, LANES)
            )

        @pl.loop(0, CH)
        def _(r):
            turn = edge_turn(c, r)
            edge_total = edge_tile(0, c)
            for i in range(1, n_frame):
                edge_total = edge_total + edge_tile(i, c)
            prepare(
                REACH + c * CH + r,
                lambda i: work_row(i, r),
                lambda i: pltpu.roll(edge_tile(i, c), turn, 1),
                pltpu.roll(edge_total, turn, 1),
            )

    def give_rows(side, c, first):
        packed = jnp.zeros((8, LANES), F32)
        for r in range(REACH):
            for i in range(n_frame):
                rows_out[side, r * n_frame + i] = work_row(i, first + r).astype(BF16)
                place = 4 * (r * n_frame + i)
                turn = lax.rem(edge_turn(c, first + r) + 2 + place, LANES)
                packed = jnp.where(
                    group == place // 4, pltpu.roll(edge_tile(i, c), turn, 1), packed
                )
        rows_out[side, REACH * n_frame] = packed.astype(BF16)

    def take_rows(side, base):
        for r in range(REACH):
            packed = rows_in[side, REACH * n_frame].astype(F32)

            def edge_of(i):
                return pltpu.roll(packed, (2 * LANES - 2 - 4 * (r * n_frame + i)) % LANES, 1)

            edge_total = edge_of(0)
            for i in range(1, n_frame):
                edge_total = edge_total + edge_of(i)
            prepare(
                base + r,
                lambda i: rows_in[side, r * n_frame + i].astype(F32),
                edge_of,
                edge_total,
            )

    def lag_row(r):
        def add(i, sums):
            centre = spread[r + REACH, i, REACH]
            return tuple(
                sums[5 * a + b] + centre * spread[r + a, i, b] for a in range(5) for b in range(5)
            )

        sums = lax.fori_loop(
            0, n_frame, add, tuple(jnp.zeros((8, LANES), F32) for _ in range(25)), unroll=4
        )
        for k in range(25):
            out[k, pl.ds(r, 1), :] = over_frames(sums[k])

    def lag_rows(first, last):
        @pl.loop(first, last)
        def _(r):
            lag_row(r)

    take_chunk(0)
    give_rows(0, 0, 0)

    @pl.when(has_above)
    def _():
        row_copy(0, above).start()

    take_chunk(chunks - 1)
    give_rows(1, chunks - 1, CH - REACH)

    @pl.when(has_below)
    def _():
        row_copy(1, below).start()

    lag_rows(REACH, CH - REACH)
    lag_rows(rows - CH + REACH, rows - REACH)

    @pl.loop(2, chunks)
    def _(step):
        c = chunk_at(step)
        take_chunk(c)
        lag_rows(c * CH + REACH, c * CH + CH + REACH)

        @pl.when(step == 2)
        def _():
            zero = jnp.zeros((REACH, n_frame, 5, 8, LANES), F32)

            @pl.when(has_below)
            def _():
                row_copy(0, below).wait_recv()
                take_rows(0, rows + REACH)

            @pl.when(jnp.logical_not(has_below))
            def _():
                spread[rows + REACH : rows + 2 * REACH] = zero

            @pl.when(has_above)
            def _():
                row_copy(1, above).wait_recv()
                take_rows(1, 0)

            @pl.when(jnp.logical_not(has_above))
            def _():
                spread[0:REACH] = zero

            lag_rows(0, REACH)
            lag_rows(rows - REACH, rows)

    lag_rows(CH - REACH, CH + REACH)

    @pl.loop(0, chunks)
    def _(c):
        @pl.loop(1, n_frame)
        def _(k):
            block_copy(c, peer(k), me).wait_send()

    @pl.loop(1, n_frame)
    def _(k):
        edge_copy(peer(k), me).wait_send()

    @pl.when(has_above)
    def _():
        row_copy(0, above).wait_send()

    @pl.when(has_below)
    def _():
        row_copy(1, below).wait_send()


def body(movie):
    frames, rows, width = movie.shape
    n_frame, n_strip = lax.axis_size("frame"), lax.axis_size("strip")
    chunks = rows // CH
    kernel = functools.partial(lag_kernel, n_frame, n_strip, 4, frames * n_frame)
    DMA = pltpu.SemaphoreType.DMA
    return pl.pallas_call(
        kernel,
        out_shape=jax.ShapeDtypeStruct((25, rows, width // n_frame), F32),
        in_specs=[pl.BlockSpec(memory_space=pl.ANY)],
        out_specs=pl.BlockSpec(memory_space=pltpu.VMEM),
        scratch_shapes=[
            pltpu.VMEM((chunks, n_frame, frames, CH, LANES), BF16),
            pltpu.VMEM((n_frame, rows // 32, 8, LANES), BF16),
            pltpu.VMEM((n_frame, rows // 32, 8, LANES), BF16),
            pltpu.VMEM((2, REACH * n_frame + 1, 8, LANES), BF16),
            pltpu.VMEM((2, REACH * n_frame + 1, 8, LANES), BF16),
            pltpu.VMEM((frames, rows, width), BF16),
            pltpu.VMEM((rows + 2 * REACH, n_frame, 5, 8, LANES), F32),
            pltpu.VMEM((frames * rows, LANES), F32),
            pltpu.VMEM((n_frame * CH * 8, LANES), F32),
            DMA((chunks, n_frame)), DMA((chunks, n_frame)), DMA((chunks,)), DMA,
            DMA((n_frame,)), DMA((n_frame,)), DMA((2,)), DMA((2,)),
        ],
        compiler_params=pltpu.CompilerParams(
            collective_id=0, has_side_effects=True, vmem_limit_bytes=56 * 2**20
        ),
        name="lag_maps",
    )(movie)


def solution(mesh):
    return jax.shard_map(
        body,
        mesh=mesh,
        in_specs=(P("frame", "strip", None),),
        out_specs=P(None, "strip", "frame"),
        check_vma=False,
    )
```

time: 432 us -> 94.2 us (0.22)
  waiting for transfers between devices: 310 us -> 0 us
  Pallas kernels: 0 us -> 91.9 us
  other arithmetic: 65.3 us -> 0 us
  local copies, waits for them, and re-layouts: 30.2 us -> 2.12 us
  between operations: 13.5 us -> 0.01 us
  starting transfers between devices: 11 us -> 0 us
    reduce_scatter x1 -> x0, waiting for transfers between devices: 159 us -> none  [body(): lax.psum_scatter(lag_products(fluctuation, rows, width), 'frame', scatter...]
    psum x1 -> x0, waiting for transfers between devices: 142 us -> none  [body(): lax.psum(jnp.sum(raw_values, axis=0).astype(jnp.bfloat16), 'frame')]
    pallas_call x0 -> x1, Pallas kernels: none -> 91.9 us  [body(): pl.pallas_call(kernel, out_shape=jax.ShapeDtypeStruct((25, rows, width //...]
    reduce_sum x3 -> x0, other arithmetic: 61.3 us -> none  [the longest x2 58.2 us: lag_products(): products.append(jnp.sum(centre * shifted, axis=0))]
    unnamed x56 -> x1, local copies, waits for them, and re-layouts: 28.1 us -> 2.12 us
    ppermute x2 -> x0, starting transfers between devices: 11 us -> none  [the longest x1 9.04 us: padded_2(): before = lax.ppermute(last, axis, up)]
    ppermute x2 -> x0, waiting for transfers between devices: 9.67 us -> none  [the longest x1 9.66 us: padded_2(): after = lax.ppermute(initial, axis, down)]
  transfers between devices with their start and end apart: 4 -> 0, of which waited for: 3 -> 0; matrix products, arithmetic and copies ran while one was open for 0% -> 0% of each run, Pallas kernels for 0% -> 0%
where the time goes in v1:
time: 94.2 us; the launch traced here: 94 us
  Pallas kernels  91.9 us (98%)
  local copies, waits for them, and re-layouts  2.12 us (2%)
    pallas_call x1, Pallas kernels, body(): pl.pallas_call(kernel, out_shape=jax.ShapeDtypeStruct((25, rows, width //...  91.9 us
    unnamed x1, local copies, waits for them, and re-layouts  2.12 us

profile of v1, /device:TPU:25, one launch (start us, length us, event | category | flops | bytes accessed | tf_op | source)
XLA Modules:
  0.0 94.0 jit_solution(428038210886843159)
XLA Ops:
  0.0 91.9 %lag_maps.1 = f32[25,64,128]{2,1,0:T(8,128)} custom-call(bf16[8,64,2048]{2,1,0:T(8,128)(2,1)} %movie.1), custom_call_target="tpu_custom_call" | custom-call | tf_op jit(solution)/shard_map/lag_maps/pallas_call | solution.py:314
  91.9 2.1 %copy.3 = f32[25,64,128]{2,1,0:T(8,128)} copy(f32[25,64,128]{2,1,0:T(8,128)} %lag_maps.1) | data formatting | bytes 1638400

commit v2 on v1

--- a/solution.py
+++ b/solution.py
@@ -96,11 +96,13 @@
     neighbours = jnp.where(has_above, 1, 0) + jnp.where(has_below, 1, 0)
     pl.semaphore_wait(barrier, n_frame - 1 + neighbours)
 
-    @pl.loop(0, chunks)
-    def _(step):
+    def send_chunk(step):
         @pl.loop(1, n_frame)
         def _(k):
             block_copy(chunk_at(step), peer(k), me).start()
+
+    send_chunk(0)
+    send_chunk(1)
 
     whole.wait()
     pick_row = lax.broadcasted_iota(jnp.int32, (width, LANES), 0)
@@ -111,7 +113,7 @@
     for f in range(frames):
         picked[pl.ds(f * rows, rows), :] = jnp.dot(held[f], pick, preferred_element_type=F32)
 
-    @pl.loop(0, rows)
+    @pl.loop(0, rows, unroll=8)
     def _(r):
         v = picked[pl.ds(r, frames, stride=rows), :]
         work[pl.ds(pl.multiple_of(r * 8, 8), 8), :] = pltpu.roll(v, 4 * lax.rem(r, 32), 1)
@@ -131,6 +133,8 @@
     def _(k):
         edge_copy(peer(k), me).start()
 
+    send_chunk(2)
+    send_chunk(3)
     edges_in[me] = edges_out[me]
 
     @pl.loop(1, n_frame)
@@ -237,6 +241,7 @@
             lag_row(r)
 
     take_chunk(0)
+    send_chunk(4)
     give_rows(0, 0, 0)
 
     @pl.when(has_above)
@@ -244,6 +249,7 @@
         row_copy(0, above).start()
 
     take_chunk(chunks - 1)
+    send_chunk(5)
     give_rows(1, chunks - 1, CH - REACH)
 
     @pl.when(has_below)
@@ -257,6 +263,11 @@
     def _(step):
         c = chunk_at(step)
         take_chunk(c)
+
+        @pl.when(step + 4 < chunks)
+        def _():
+            send_chunk(step + 4)
+
         lag_rows(c * CH + REACH, c * CH + CH + REACH)
 
         @pl.when(step == 2)

time: 94.2 us -> 71.9 us (0.76); the launches traced: 94 us -> 70.7 us
  Pallas kernels: 91.9 us -> 68.6 us
    pallas_call x1, Pallas kernels: 91.9 us -> 68.6 us  [body(): pl.pallas_call(kernel, out_shape=jax.ShapeDtypeStruct((25, rows, width //...]
where the time goes in v2:
time: 71.9 us; the launch traced here: 70.7 us
  Pallas kernels  68.6 us (95%)
  local copies, waits for them, and re-layouts  2.12 us (3%)
    pallas_call x1, Pallas kernels, body(): pl.pallas_call(kernel, out_shape=jax.ShapeDtypeStruct((25, rows, width //...  68.6 us
    unnamed x1, local copies, waits for them, and re-layouts  2.12 us

profile of v2, /device:TPU:25, one launch (start us, length us, event | category | flops | bytes accessed | tf_op | source)
XLA Modules:
  0.0 70.7 jit_solution(16374437211296272312)
XLA Ops:
  0.0 68.6 %lag_maps.1 = f32[25,64,128]{2,1,0:T(8,128)} custom-call(bf16[8,64,2048]{2,1,0:T(8,128)(2,1)} %movie.1), custom_call_target="tpu_custom_call" | custom-call | tf_op jit(solution)/shard_map/lag_maps/pallas_call | solution.py:325
  68.6 2.1 %copy.3 = f32[25,64,128]{2,1,0:T(8,128)} copy(f32[25,64,128]{2,1,0:T(8,128)} %lag_maps.1) | data formatting | bytes 1638400

commit v3 on v1

--- a/solution.py
+++ b/solution.py
@@ -45,21 +45,27 @@
         return pltpu.make_async_remote_copy(
             src_ref=movie.at[:, pl.ds(pl.multiple_of(c * CH, CH), CH), columns(g)],
             dst_ref=block.at[c, source],
-            send_sem=send_sem.at[c, g], recv_sem=recv_sem.at[c, source],
+            send_sem=send_sem, recv_sem=recv_sem.at[c],
             device_id={"frame": g}, device_id_type=MESH,
         )
 
     def own_copy(c):
         return pltpu.make_async_copy(
             movie.at[:, pl.ds(pl.multiple_of(c * CH, CH), CH), columns(me)],
-            block.at[c, me], own_sem.at[c],
+            block.at[c, me], own_sem,
         )
 
     def edge_copy(g, source):
         return pltpu.make_async_remote_copy(
             src_ref=edges_out.at[g], dst_ref=edges_in.at[source],
-            send_sem=edge_send.at[g], recv_sem=edge_recv.at[source],
+            send_sem=edge_send, recv_sem=edge_recv,
             device_id={"frame": g}, device_id_type=MESH,
+        )
+
+    def all_of(ref, sent, received):
+        return pltpu.make_async_remote_copy(
+            src_ref=ref, dst_ref=ref, send_sem=sent, recv_sem=received,
+            device_id={"frame": peer(1)}, device_id_type=MESH,
         )
 
     def row_copy(side, to):
@@ -92,15 +98,6 @@
     @pl.when(has_below)
     def _():
         pl.semaphore_signal(barrier, inc=1, device_id={"strip": below}, device_id_type=MESH)
-
-    neighbours = jnp.where(has_above, 1, 0) + jnp.where(has_below, 1, 0)
-    pl.semaphore_wait(barrier, n_frame - 1 + neighbours)
-
-    @pl.loop(0, chunks)
-    def _(step):
-        @pl.loop(1, n_frame)
-        def _(k):
-            block_copy(chunk_at(step), peer(k), me).start()
 
     whole.wait()
     pick_row = lax.broadcasted_iota(jnp.int32, (width, LANES), 0)
@@ -111,7 +108,7 @@
     for f in range(frames):
         picked[pl.ds(f * rows, rows), :] = jnp.dot(held[f], pick, preferred_element_type=F32)
 
-    @pl.loop(0, rows)
+    @pl.loop(0, rows, unroll=8)
     def _(r):
         v = picked[pl.ds(r, frames, stride=rows), :]
         work[pl.ds(pl.multiple_of(r * 8, 8), 8), :] = pltpu.roll(v, 4 * lax.rem(r, 32), 1)
@@ -127,15 +124,28 @@
                 packed = jnp.where(group == lax.rem(r + g, 32), v, packed)
             edges_out[g, q] = pltpu.roll(packed, lax.rem(LANES - 4 * g, LANES), 1).astype(BF16)
 
+    neighbours = jnp.where(has_above, 1, 0) + jnp.where(has_below, 1, 0)
+    pl.semaphore_wait(barrier, n_frame - 1 + neighbours)
+
+    def send_chunk(step):
+        @pl.loop(1, n_frame)
+        def _(k):
+            block_copy(chunk_at(step), peer(k), me).start()
+
+
     @pl.loop(1, n_frame)
     def _(k):
         edge_copy(peer(k), me).start()
 
+    send_chunk(0)
+    send_chunk(1)
+    send_chunk(2)
+    send_chunk(3)
     edges_in[me] = edges_out[me]
 
-    @pl.loop(1, n_frame)
-    def _(k):
-        edge_copy(me, peer(k)).wait_recv()
+    @pl.loop(0, chunks)
+    def _(c):
+        own_copy(c).wait()
 
     beside = ((lane >= LANES - 2) & has_left) | ((lane < 2) & has_right)
 
@@ -165,16 +175,23 @@
     def edge_tile(i, c):
         return edges_in[i, c // (32 // CH)].astype(F32)
 
-    def take_chunk(c):
-        @pl.loop(1, n_frame)
-        def _(k):
-            block_copy(c, me, peer(k)).wait_recv()
-
-        own_copy(c).wait()
+    def take_chunk(step):
+        c = chunk_at(step)
+
+        all_of(block.at[c, pl.ds(0, n_frame - 1)], send_sem, recv_sem.at[c]).wait_recv()
+
+        @pl.when(step + 4 < chunks)
+        def _():
+            send_chunk(step + 4)
+
         for i in range(n_frame):
             work[pl.ds(i * CH * 8, CH * 8), :] = (
                 block[c, i].astype(F32).reshape(CH * 8, LANES)
             )
+
+        @pl.when(step == 0)
+        def _():
+            all_of(edges_in.at[pl.ds(0, n_frame - 1)], edge_send, edge_recv).wait_recv()
 
         @pl.loop(0, CH)
         def _(r):
@@ -243,7 +260,7 @@
     def _():
         row_copy(0, above).start()
 
-    take_chunk(chunks - 1)
+    take_chunk(1)
     give_rows(1, chunks - 1, CH - REACH)
 
     @pl.when(has_below)
@@ -256,7 +273,8 @@
     @pl.loop(2, chunks)
     def _(step):
         c = chunk_at(step)
-        take_chunk(c)
+        take_chunk(step)
+
         lag_rows(c * CH + REACH, c * CH + CH + REACH)
 
         @pl.when(step == 2)
@@ -286,15 +304,8 @@
 
     lag_rows(CH - REACH, CH + REACH)
 
-    @pl.loop(0, chunks)
-    def _(c):
-        @pl.loop(1, n_frame)
-        def _(k):
-            block_copy(c, peer(k), me).wait_send()
-
-    @pl.loop(1, n_frame)
-    def _(k):
-        edge_copy(peer(k), me).wait_send()
+    all_of(block.at[:, pl.ds(0, n_frame - 1)], send_sem, recv_sem.at[0]).wait_send()
+    all_of(edges_in.at[pl.ds(0, n_frame - 1)], edge_send, edge_recv).wait_send()
 
     @pl.when(has_above)
     def _():
@@ -326,8 +337,8 @@
             pltpu.VMEM((rows + 2 * REACH, n_frame, 5, 8, LANES), F32),
             pltpu.VMEM((frames * rows, LANES), F32),
             pltpu.VMEM((n_frame * CH * 8, LANES), F32),
-            DMA((chunks, n_frame)), DMA((chunks, n_frame)), DMA((chunks,)), DMA,
-            DMA((n_frame,)), DMA((n_frame,)), DMA((2,)), DMA((2,)),
+            DMA, DMA((chunks,)), DMA, DMA,
+            DMA, DMA, DMA((2,)), DMA((2,)),
         ],
         compiler_params=pltpu.CompilerParams(
             collective_id=0, has_side_effects=True, vmem_limit_bytes=56 * 2**20

time: 94.2 us -> 66.9 us (0.71); the launches traced: 94 us -> 65.7 us
  Pallas kernels: 91.9 us -> 63.5 us
    pallas_call x1, Pallas kernels: 91.9 us -> 63.5 us  [body(): pl.pallas_call(kernel, out_shape=jax.ShapeDtypeStruct((25, rows, width //...]
where the time goes in v3:
time: 66.9 us; the launch traced here: 65.7 us
  Pallas kernels  63.5 us (95%)
  local copies, waits for them, and re-layouts  2.12 us (3%)
    pallas_call x1, Pallas kernels, body(): pl.pallas_call(kernel, out_shape=jax.ShapeDtypeStruct((25, rows, width //...  63.5 us
    unnamed x1, local copies, waits for them, and re-layouts  2.12 us

profile of v3, /device:TPU:25, one launch (start us, length us, event | category | flops | bytes accessed | tf_op | source)
XLA Modules:
  0.0 65.7 jit_solution(4223757656577029489)
XLA Ops:
  0.0 63.5 %lag_maps.1 = f32[25,64,128]{2,1,0:T(8,128)} custom-call(bf16[8,64,2048]{2,1,0:T(8,128)(2,1)} %movie.1), custom_call_target="tpu_custom_call" | custom-call | tf_op jit(solution)/shard_map/lag_maps/pallas_call | solution.py:325
  63.5 2.1 %copy.3 = f32[25,64,128]{2,1,0:T(8,128)} copy(f32[25,64,128]{2,1,0:T(8,128)} %lag_maps.1) | data formatting | bytes 1638400

commit v4 on v3

v4 whole, which is shorter than its diff:
```python
import functools

import jax
import jax.numpy as jnp
from jax import lax
from jax.experimental import pallas as pl
from jax.experimental.pallas import tpu as pltpu
from jax.sharding import PartitionSpec as P

MESH = pl.DeviceIdType.MESH
LANES = 128
CH = 8
REACH = 2
AHEAD = 4
WRAP = 0
F32 = jnp.float32
BF16 = jnp.bfloat16


def lag_kernel(
    n_frame, n_strip, n_x, frames_total,
    movie, out,
    block, edges_in, edges_out, rows_in, rows_out, held, spread, picked, work,
    reduced, sent, got, means, far_means, totals,
    send_sem, recv_sem, own_sem, held_sem, edge_send, edge_recv, row_send, row_recv,
    part_send, part_recv,
):
    frames, rows, width = movie.shape
    chunks = rows // CH
    n_half = n_frame // 2
    me = lax.axis_index("frame")
    strip = lax.axis_index("strip")
    first = (me // n_half) * n_half
    mine = me - first
    partner = lax.rem(me + n_half, n_frame)
    inverse = 1.0 / frames_total

    lane = lax.broadcasted_iota(jnp.int32, (8, LANES), 1)
    sub = lax.broadcasted_iota(jnp.int32, (8, LANES), 0)
    group = lane // 4
    zero = jnp.zeros((8, LANES), F32)

    def peer(k):
        dx, dz = k // 2, lax.rem(k, 2)
        return lax.rem(mine // n_x + dz, 2) * n_x + lax.rem(lax.rem(mine, n_x) + dx, n_x)

    def chunk_at(step):
        return lax.rem(chunks - step, chunks)

    def owner(slot, index):
        return lax.rem(first + index + (1 - slot) * n_half, n_frame)

    def tile(c, g):
        return movie.at[
            :, pl.ds(pl.multiple_of(c * CH, CH), CH),
            pl.ds(pl.multiple_of(g * LANES, LANES), LANES),
        ]

    def own_copy(c, slot):
        return pltpu.make_async_copy(tile(c, owner(slot, mine)), block.at[c, slot, mine], own_sem)

    def to_peer(src, dst, send, recv, index):
        return pltpu.make_async_remote_copy(
            src_ref=src, dst_ref=dst, send_sem=send, recv_sem=recv,
            device_id={"frame": first + index}, device_id_type=MESH,
        )

    def all_of(ref, send, recv):
        return to_peer(ref, ref, send, recv, peer(1))

    def to_partner(at, count):
        return pltpu.make_async_remote_copy(
            src_ref=sent.at[pl.ds(at, count)], dst_ref=got.at[pl.ds(at, count)],
            send_sem=part_send, recv_sem=part_recv.at[at],
            device_id={"frame": partner}, device_id_type=MESH,
        )

    def row_copy(side, to):
        return pltpu.make_async_remote_copy(
            src_ref=rows_out.at[side], dst_ref=rows_in.at[side],
            send_sem=row_send.at[side], recv_sem=row_recv.at[side],
            device_id={"strip": to}, device_id_type=MESH,
        )

    above, below = jnp.maximum(strip - 1, 0), jnp.minimum(strip + 1, n_strip - 1)
    has_above, has_below = strip > 0, strip < n_strip - 1

    whole = pltpu.make_async_copy(movie, held, held_sem)
    whole.start()

    @pl.loop(0, chunks)
    def _(c):
        own_copy(c, 0).start()
        own_copy(c, 1).start()

    barrier = pltpu.get_barrier_semaphore()

    @pl.loop(1, n_half)
    def _(k):
        pl.semaphore_signal(
            barrier, inc=1, device_id={"frame": first + peer(k)}, device_id_type=MESH
        )

    pl.semaphore_signal(barrier, inc=1, device_id={"frame": partner}, device_id_type=MESH)

    @pl.when(has_above)
    def _():
        pl.semaphore_signal(barrier, inc=1, device_id={"strip": above}, device_id_type=MESH)

    @pl.when(has_below)
    def _():
        pl.semaphore_signal(barrier, inc=1, device_id={"strip": below}, device_id_type=MESH)

    totals[...] = jnp.zeros(totals.shape, F32)
    means[...] = jnp.zeros(means.shape, F32)

    whole.wait()
    pick_row = lax.broadcasted_iota(jnp.int32, (width, LANES), 0)
    pick_lane = lax.broadcasted_iota(jnp.int32, (width, LANES), 1)
    j = lax.rem(pick_lane, 4)
    target = (pick_lane // 4) * LANES + jnp.where(j < 2, j - 2, LANES - 2 + j)
    pick = jnp.where((pick_row == target) & (pick_lane < 4 * n_frame), 1.0, 0.0).astype(BF16)
    for f in range(frames):
        picked[pl.ds(f * rows, rows), :] = jnp.dot(held[f], pick, preferred_element_type=F32)

    @pl.loop(0, rows, unroll=8)
    def _(r):
        v = picked[pl.ds(r, frames, stride=rows), :]
        work[pl.ds(pl.multiple_of(r * 8, 8), 8), :] = pltpu.roll(v, 4 * lax.rem(r, 32), 1)

    @pl.loop(0, n_frame)
    def _(g):
        for q in range(rows // 32):
            packed = zero
            for r in range(32):
                v = work[pl.ds((q * 32 + r) * 8, 8), :]
                packed = jnp.where(group == lax.rem(r + g, 32), v, packed)
            edges_out[g, q] = pltpu.roll(packed, lax.rem(LANES - 4 * g, LANES), 1).astype(BF16)

    neighbours = jnp.where(has_above, 1, 0) + jnp.where(has_below, 1, 0)
    pl.semaphore_wait(barrier, n_half + neighbours)

    def send_chunk(step):
        c = chunk_at(step)

        @pl.loop(1, n_half)
        def _(k):
            p = peer(k)
            for slot in range(2):
                to_peer(
                    tile(c, owner(slot, p)), block.at[c, slot, mine],
                    send_sem, recv_sem.at[c], p,
                ).start()

    @pl.loop(1, n_half)
    def _(k):
        p = peer(k)
        for slot in range(2):
            to_peer(
                edges_out.at[owner(slot, p)], edges_in.at[slot, mine], edge_send, edge_recv, p
            ).start()

    for step in range(AHEAD):
        send_chunk(step)
    for slot in range(2):
        edges_in[slot, mine] = edges_out[owner(slot, mine)]

    @pl.loop(0, chunks)
    def _(c):
        own_copy(c, 0).wait()
        own_copy(c, 1).wait()

    beside = []
    for slot in range(2):
        g = owner(slot, mine)
        beside.append(((lane >= LANES - 2) & (g > 0)) | ((lane < 2) & (g < n_frame - 1)))

    def shifted(value, edge, b):
        if b == 0:
            return value
        near = lane < b if b > 0 else lane >= LANES + b
        return pltpu.roll(jnp.where(near, edge, value), (LANES - b) % LANES, 1)

    def over_frames(total):
        return jnp.sum(total, axis=0, keepdims=True) * (1.0 / (n_half * frames))

    def prepare(slot, r, row_of, edge_of, edge_total):
        total = row_of(0)
        for i in range(1, n_half):
            total = total + row_of(i)
        mean, edge_mean = over_frames(total), over_frames(edge_total)
        means[slot, 0, pl.ds(r + 8, 1), :] = mean
        means[slot, 1, pl.ds(r + 8, 1), :] = jnp.where(beside[slot][:1], edge_mean, 0.0)
        for i in range(n_half):
            value = row_of(i) - mean
            edge = jnp.where(beside[slot], edge_of(i) - edge_mean, 0.0)
            for b in range(-REACH, REACH + 1):
                spread[slot, r + REACH, i, b + REACH] = shifted(value, edge, b)

    def work_row(slot, i, r):
        return work[pl.ds((slot * n_half + i) * CH * 8 + r, 8, stride=CH), :]

    def edge_turn(c, r):
        return lax.rem(2 * LANES - 2 - 4 * (lax.rem(c, 32 // CH) * CH + r), LANES)

    def edge_tile(slot, i, c):
        return edges_in[slot, i, c // (32 // CH)].astype(F32)

    def take_chunk(step):
        c = chunk_at(step)
        all_of(block.at[c, :, pl.ds(0, n_half - 1)], send_sem, recv_sem.at[c]).wait_recv()

        @pl.when(step + AHEAD < chunks)
        def _():
            send_chunk(step + AHEAD)

        for slot in range(2):
            for i in range(n_half):
                work[pl.ds((slot * n_half + i) * CH * 8, CH * 8), :] = (
                    block[c, slot, i].astype(F32).reshape(CH * 8, LANES)
                )

        @pl.when(step == 0)
        def _():
            all_of(edges_in.at[:, pl.ds(0, n_half - 1)], edge_send, edge_recv).wait_recv()

        edge_totals = []
        for slot in range(2):
            edge_total = edge_tile(slot, 0, c)
            for i in range(1, n_half):
                edge_total = edge_total + edge_tile(slot, i, c)
            edge_totals.append(edge_total)

        @pl.loop(0, CH, unroll=2)
        def _(r):
            turn = edge_turn(c, r)
            for slot in range(2):
                prepare(
                    slot, c * CH + r,
                    lambda i: work_row(slot, i, r),
                    lambda i: pltpu.roll(edge_tile(slot, i, c), turn, 1),
                    pltpu.roll(edge_totals[slot], turn, 1),
                )

    def place(slot, r, i):
        return (slot * REACH + r) * n_half + i

    def give_rows(side, c, start):
        packed = zero
        for slot in range(2):
            for r in range(REACH):
                for i in range(n_half):
                    at = place(slot, r, i)
                    rows_out[side, at] = work_row(slot, i, start + r).astype(BF16)
                    turn = lax.rem(edge_turn(c, start + r) + 2 + 4 * at, LANES)
                    packed = jnp.where(
                        group == at, pltpu.roll(edge_tile(slot, i, c), turn, 1), packed
                    )
        rows_out[side, 2 * REACH * n_half] = packed.astype(BF16)

    def take_rows(side, base):
        packed = rows_in[side, 2 * REACH * n_half].astype(F32)
        for slot in range(2):
            for r in range(REACH):

                def edge_of(i):
                    turn = (2 * LANES - 2 - 4 * place(slot, r, i)) % LANES
                    return pltpu.roll(packed, turn, 1)

                edge_total = edge_of(0)
                for i in range(1, n_half):
                    edge_total = edge_total + edge_of(i)
                prepare(
                    slot, base + r,
                    lambda i: rows_in[side, place(slot, r, i)].astype(F32),
                    edge_of, edge_total,
                )

    def lag_group(slot, start):
        @pl.loop(0, CH)
        def _(n):
            r = lax.rem(start + n, rows)
            sums = [None] * 25
            for i in range(n_half):
                centre = spread[slot, r + REACH, i, REACH]
                for k in range(25):
                    term = centre * spread[slot, r + k // 5, i, k % 5]
                    sums[k] = term if i == 0 else sums[k] + term
            for k in range(25):
                reduced[k, pl.ds(pl.multiple_of(n * 8, 8), 8), :] = sums[k]

    def lag_plane(k):
        total = reduced[k, pl.ds(0, CH, stride=8), :]
        for n in range(1, 8):
            total = total + reduced[k, pl.ds(n, CH, stride=8), :]
        return total * inverse

    def pack_planes(at):
        for p in range(13):
            sent[at, p] = lag_plane(12 + p)
        side = zero
        for k in range(12):
            plane = lag_plane(k)
            if k % 5 != REACH:
                side = jnp.where(group == k, pltpu.roll(plane, 4 * k + 2, 1), side)
            if at is WRAP:
                sent[at + 1, k] = plane
        sent[at, 13] = side

    def mean_rows(c):
        return pl.ds(pl.multiple_of(8 + c * CH, CH), CH)

    def send_group(at, c):
        lag_group(0, c * CH + REACH)
        pack_planes(at)
        for kind in range(2):
            sent[at, 14 + kind] = means[0, kind, mean_rows(c), :]
        to_partner(at, 1).start()

    def send_wrap():
        lag_group(0, rows - CH + REACH)
        pack_planes(WRAP)
        for kind in range(2):
            sent[WRAP, 14 + kind] = means[0, kind, mean_rows(0), :]
            sent[WRAP + 1, 12 + kind] = means[0, kind, mean_rows(chunks - 1), :]
            sent[WRAP + 1, 14 + kind] = (
                means[0, kind, pl.ds(0, 8), :] + means[0, kind, pl.ds(8 + rows, 8), :]
            )
        to_partner(WRAP, 2).start()

    def add(k, at, value, keep=None):
        if keep is not None:
            value = jnp.where(keep, value, 0.0)
        totals[k, pl.ds(at, 8), :] += value

    wrapped = ((rows - CH + REACH, sub < CH - REACH), (REACH - CH, sub >= CH - REACH))

    def own_group(c):
        lag_group(1, c * CH + REACH)
        for k in range(25):
            add(k, 8 + c * CH + REACH, lag_plane(k))

    def own_wrap():
        lag_group(1, rows - CH + REACH)
        for k in range(25):
            plane = lag_plane(k)
            for start, keep in wrapped:
                add(k, 8 + start, plane, keep)

    def add_far(at, base, keep=None):
        gap = {}
        for a in range(-REACH, REACH + 1):
            value, edge = (
                means[1, kind, pl.ds(base + a, 8), :] - far_means[kind, pl.ds(base + a, 8), :]
                for kind in range(2)
            )
            for b in range(-REACH, REACH + 1):
                gap[a, b] = shifted(value, edge, b)
        centre = gap[0, 0] * 0.25
        side = got[at, 13]
        for k in range(25):
            a, b = k // 5 - REACH, k % 5 - REACH
            value = centre * gap[a, b]
            if k >= 12:
                plane = got[at, k - 12]
                value = value + plane
                if k > 12:
                    moved = pltpu.roll(plane, b % LANES, 1)
                    inside = (lane >= b) & (lane < LANES + b)
                    add(24 - k, base + a, jnp.where(inside, moved, 0.0), keep)
            else:
                if b != 0:
                    column = pltpu.roll(side, (2 * LANES - 4 * k - 2) % LANES, 1)
                    outside = (lane < -b) | (lane >= LANES - b)
                    if keep is not None:
                        outside = outside & (sub != 6 if a == -1 else sub < 6) if a < 0 else outside
                    value = value + jnp.where(outside, column, 0.0)
                if keep is not None and a < 0:
                    direct = sub == 6 if a == -1 else sub >= 6
                    value = value + jnp.where(direct, got[at + 1, k], 0.0)
            add(k, base, value, keep)

    def take_group(at, c):
        to_partner(at, 1).wait_recv()
        for kind in range(2):
            far_means[kind, mean_rows(c), :] = got[at, 14 + kind]
        add_far(at, 8 + c * CH + REACH)

    def take_wrap():
        to_partner(WRAP, 2).wait_recv()
        for kind in range(2):
            far_means[kind, mean_rows(0), :] = got[WRAP, 14 + kind]
            far_means[kind, mean_rows(chunks - 1), :] = got[WRAP + 1, 12 + kind]
            ends = got[WRAP + 1, 14 + kind]
            far_means[kind, pl.ds(0, 8), :] = jnp.where(sub >= 8 - REACH, ends, 0.0)
            far_means[kind, pl.ds(8 + rows, 8), :] = jnp.where(sub < REACH, ends, 0.0)
        for start, keep in wrapped:
            add_far(WRAP, 8 + start, keep)

    take_chunk(0)
    give_rows(0, 0, 0)

    @pl.when(has_above)
    def _():
        row_copy(0, above).start()

    take_chunk(1)
    give_rows(1, chunks - 1, CH - REACH)

    @pl.when(has_below)
    def _():
        row_copy(1, below).start()

    @pl.loop(2, chunks - 1)
    def _(step):
        c = chunk_at(step)
        take_chunk(step)

        @pl.when(step == 3)
        def _():
            empty = jnp.zeros((2, REACH, n_half, 5, 8, LANES), F32)

            @pl.when(has_below)
            def _():
                row_copy(0, below).wait_recv()
                take_rows(0, rows)

            @pl.when(jnp.logical_not(has_below))
            def _():
                spread[:, rows + REACH : rows + 2 * REACH] = empty

            @pl.when(has_above)
            def _():
                row_copy(1, above).wait_recv()
                take_rows(1, -REACH)

            @pl.when(jnp.logical_not(has_above))
            def _():
                spread[:, 0:REACH] = empty

            send_wrap()

        send_group(step, c)
        own_group(c)

        @pl.when(step == 3)
        def _():
            own_wrap()

        @pl.when(step == 4)
        def _():
            take_wrap()

        @pl.when(step >= 4)
        def _():
            take_group(step - 2, chunk_at(step - 2))

    last = chunks - 1
    take_chunk(last)
    send_group(last, 1)
    send_group(last + 1, 0)
    own_group(1)
    take_group(last - 2, 3)
    take_group(last - 1, 2)
    own_group(0)
    take_group(last, 1)
    take_group(last + 1, 0)
    out[...] = totals[:, 8 : 8 + rows, :]

    all_of(block.at[:, :, pl.ds(0, n_half - 1)], send_sem, recv_sem.at[0]).wait_send()
    all_of(edges_in.at[:, pl.ds(0, n_half - 1)], edge_send, edge_recv).wait_send()
    to_partner(0, chunks + 1).wait_send()

    @pl.when(has_above)
    def _():
        row_copy(0, above).wait_send()

    @pl.when(has_below)
    def _():
        row_copy(1, below).wait_send()


def body(movie):
    frames, rows, width = movie.shape
    n_frame, n_strip = lax.axis_size("frame"), lax.axis_size("strip")
    chunks, n_half = rows // CH, n_frame // 2
    kernel = functools.partial(lag_kernel, n_frame, n_strip, 4, frames * n_frame)
    DMA = pltpu.SemaphoreType.DMA
    padded = rows + 16
    return pl.pallas_call(
        kernel,
        out_shape=jax.ShapeDtypeStruct((25, rows, width // n_frame), F32),
        in_specs=[pl.BlockSpec(memory_space=pl.ANY)],
        out_specs=pl.BlockSpec(memory_space=pltpu.VMEM),
        scratch_shapes=[
            pltpu.VMEM((chunks, 2, n_half, frames, CH, LANES), BF16),
            pltpu.VMEM((2, n_half, rows // 32, 8, LANES), BF16),
            pltpu.VMEM((n_frame, rows // 32, 8, LANES), BF16),
            pltpu.VMEM((2, 2 * REACH * n_half + 1, 8, LANES), BF16),
            pltpu.VMEM((2, 2 * REACH * n_half + 1, 8, LANES), BF16),
            pltpu.VMEM((frames, rows, width), BF16),
            pltpu.VMEM((2, rows + 2 * REACH, n_half, 5, 8, LANES), F32),
            pltpu.VMEM((frames * rows, LANES), F32),
            pltpu.VMEM((n_frame * CH * 8, LANES), F32),
            pltpu.VMEM((25, CH * 8, LANES), F32),
            pltpu.VMEM((chunks + 1, 16, 8, LANES), F32),
            pltpu.VMEM((chunks + 1, 16, 8, LANES), F32),
            pltpu.VMEM((2, 2, padded, LANES), F32),
            pltpu.VMEM((2, padded, LANES), F32),
            pltpu.VMEM((25, padded, LANES), F32),
            DMA, DMA((chunks,)), DMA, DMA, DMA, DMA, DMA((2,)), DMA((2,)),
            DMA, DMA((chunks + 1,)),
        ],
        compiler_params=pltpu.CompilerParams(
            collective_id=0, has_side_effects=True, vmem_limit_bytes=56 * 2**20
        ),
        name="lag_maps",
    )(movie)


def solution(mesh):
    return jax.shard_map(
        body,
        mesh=mesh,
        in_specs=(P("frame", "strip", None),),
        out_specs=P(None, "strip", "frame"),
        check_vma=False,
    )
```

time: 66.9 us -> 61.7 us (0.922)
  Pallas kernels: 63.5 us -> 58.3 us
    pallas_call x1, Pallas kernels: 63.5 us -> 58.3 us  [body(): pl.pallas_call(kernel, out_shape=jax.ShapeDtypeStruct((25, rows, width //...]
where the time goes in v4:
time: 61.7 us; the launch traced here: 60.4 us
  Pallas kernels  58.3 us (94%)
  local copies, waits for them, and re-layouts  2.12 us (3%)
    pallas_call x1, Pallas kernels, body(): pl.pallas_call(kernel, out_shape=jax.ShapeDtypeStruct((25, rows, width //...  58.3 us
    unnamed x1, local copies, waits for them, and re-layouts  2.12 us

profile of v4, /device:TPU:25, one launch (start us, length us, event | category | flops | bytes accessed | tf_op | source)
XLA Modules:
  0.0 60.4 jit_solution(12798637047330151202)
XLA Ops:
  0.0 58.3 %lag_maps.1 = f32[25,64,128]{2,1,0:T(8,128)} custom-call(bf16[8,64,2048]{2,1,0:T(8,128)(2,1)} %movie.1), custom_call_target="tpu_custom_call" | custom-call | tf_op jit(solution)/shard_map/lag_maps/pallas_call | solution.py:490
  58.3 2.1 %copy.3 = f32[25,64,128]{2,1,0:T(8,128)} copy(f32[25,64,128]{2,1,0:T(8,128)} %lag_maps.1) | data formatting | bytes 1638400

commit v5 on v4

--- a/solution.py
+++ b/solution.py
@@ -11,7 +11,7 @@
 LANES = 128
 CH = 8
 REACH = 2
-AHEAD = 4
+AHEAD = 2
 WRAP = 0
 F32 = jnp.float32
 BF16 = jnp.bfloat16
@@ -447,22 +447,18 @@
         def _():
             own_wrap()
 
-        @pl.when(step == 4)
-        def _():
-            take_wrap()
-
-        @pl.when(step >= 4)
-        def _():
-            take_group(step - 2, chunk_at(step - 2))
-
     last = chunks - 1
     take_chunk(last)
     send_group(last, 1)
     send_group(last + 1, 0)
     own_group(1)
-    take_group(last - 2, 3)
-    take_group(last - 1, 2)
     own_group(0)
+    take_wrap()
+
+    @pl.loop(2, last)
+    def _(step):
+        take_group(step, chunk_at(step))
+
     take_group(last, 1)
     take_group(last + 1, 0)
     out[...] = totals[:, 8 : 8 + rows, :]

time: 61.7 us -> 56.3 us (0.912)
  the two profiles are of different devices: /device:TPU:25 before, /device:TPU:24 now
where the time goes in v5:
time: 56.3 us; the launch traced here: 56.2 us
  Pallas kernels  54.1 us (96%)
  local copies, waits for them, and re-layouts  2.12 us (4%)
    pallas_call x1, Pallas kernels, body(): pl.pallas_call(kernel, out_shape=jax.ShapeDtypeStruct((25, rows, width //...  54.1 us
    unnamed x1, local copies, waits for them, and re-layouts  2.12 us

profile of v5, /device:TPU:24, one launch (start us, length us, event | category | flops | bytes accessed | tf_op | source)
XLA Modules:
  0.0 56.2 jit_solution(9257886776025089349)
XLA Ops:
  0.0 54.1 %lag_maps.1 = f32[25,64,128]{2,1,0:T(8,128)} custom-call(bf16[8,64,2048]{2,1,0:T(8,128)(2,1)} %movie.1), custom_call_target="tpu_custom_call" | custom-call | tf_op jit(solution)/shard_map/lag_maps/pallas_call | solution.py:486
  54.1 2.1 %copy.3 = f32[25,64,128]{2,1,0:T(8,128)} copy(f32[25,64,128]{2,1,0:T(8,128)} %lag_maps.1) | data formatting | bytes 1638400

commit v6 on v5

--- a/solution.py
+++ b/solution.py
@@ -11,8 +11,7 @@
 LANES = 128
 CH = 8
 REACH = 2
-AHEAD = 2
-WRAP = 0
+AHEAD = 3
 F32 = jnp.float32
 BF16 = jnp.bfloat16
 
@@ -68,10 +67,11 @@
     def all_of(ref, send, recv):
         return to_peer(ref, ref, send, recv, peer(1))
 
-    def to_partner(at, count):
+    def to_partner(m, count):
+        at = 16 * m
         return pltpu.make_async_remote_copy(
             src_ref=sent.at[pl.ds(at, count)], dst_ref=got.at[pl.ds(at, count)],
-            send_sem=part_send, recv_sem=part_recv.at[at],
+            send_sem=part_send, recv_sem=part_recv.at[m],
             device_id={"frame": partner}, device_id_type=MESH,
         )
 
@@ -276,10 +276,10 @@
                     edge_of, edge_total,
                 )
 
-    def lag_group(slot, start):
+    def lag_group(slot, row_at):
         @pl.loop(0, CH)
         def _(n):
-            r = lax.rem(start + n, rows)
+            r = row_at(n)
             sums = [None] * 25
             for i in range(n_half):
                 centre = spread[slot, r + REACH, i, REACH]
@@ -295,59 +295,81 @@
             total = total + reduced[k, pl.ds(n, CH, stride=8), :]
         return total * inverse
 
-    def pack_planes(at):
+    def mean_rows(c):
+        return pl.ds(pl.multiple_of(8 + c * CH, CH), CH)
+
+    def put(value, g):
+        return pltpu.roll(value, (4 * g + 2) % LANES, 1)
+
+    def unput(value, g):
+        return pltpu.roll(value, (2 * LANES - 4 * g - 2) % LANES, 1)
+
+    def plain(c):
+        start = c * CH + REACH
+        return (lambda n: start + n), ((start, None),)
+
+    def inner_ends():
+        return (
+            lambda n: jnp.where(n < 4, rows - CH + REACH + n, n - REACH),
+            ((rows - CH + REACH, sub < 4), (-REACH, sub >= 4)),
+        )
+
+    def outer_ends():
+        return (
+            lambda n: jnp.where(n < 4, CH - REACH + n, lax.rem(rows - CH + REACH + n, rows)),
+            (
+                (CH - REACH, sub < 4),
+                (rows - CH + REACH, (sub >= 4) & (sub < 6)),
+                (REACH - CH, sub >= 6),
+            ),
+        )
+
+    def send_group(m, row_at, chunk_means, ends=False):
+        at = 16 * m
+        lag_group(0, row_at)
         for p in range(13):
-            sent[at, p] = lag_plane(12 + p)
-        side = zero
+            sent[at + p] = lag_plane(12 + p)
+        side, low = zero, [zero] * 3
         for k in range(12):
+            if k % 5 == REACH and not ends:
+                continue
             plane = lag_plane(k)
             if k % 5 != REACH:
-                side = jnp.where(group == k, pltpu.roll(plane, 4 * k + 2, 1), side)
-            if at is WRAP:
-                sent[at + 1, k] = plane
-        sent[at, 13] = side
-
-    def mean_rows(c):
-        return pl.ds(pl.multiple_of(8 + c * CH, CH), CH)
-
-    def send_group(at, c):
-        lag_group(0, c * CH + REACH)
-        pack_planes(at)
-        for kind in range(2):
-            sent[at, 14 + kind] = means[0, kind, mean_rows(c), :]
-        to_partner(at, 1).start()
-
-    def send_wrap():
-        lag_group(0, rows - CH + REACH)
-        pack_planes(WRAP)
-        for kind in range(2):
-            sent[WRAP, 14 + kind] = means[0, kind, mean_rows(0), :]
-            sent[WRAP + 1, 12 + kind] = means[0, kind, mean_rows(chunks - 1), :]
-            sent[WRAP + 1, 14 + kind] = (
-                means[0, kind, pl.ds(0, 8), :] + means[0, kind, pl.ds(8 + rows, 8), :]
-            )
-        to_partner(WRAP, 2).start()
+                side = jnp.where(group == k, put(plane, k), side)
+            if ends:
+                place = 2 * (k % 4)
+                low[k // 4] = jnp.where(
+                    sub // 2 == k % 4, pltpu.roll(plane, (place + 2) % 8, 0), low[k // 4]
+                )
+        for n, (mean, edge) in enumerate(chunk_means):
+            sent[at + 14 + n] = mean
+            side = jnp.where(group == 12 + n, put(edge, 12 + n), side)
+        sent[at + 13] = side
+        if ends:
+            for n in range(3):
+                sent[at + 15 + n] = low[n]
+        to_partner(m, planes(len(chunk_means), ends)).start()
+
+    def planes(n_means, ends=False):
+        return 14 + n_means + (3 if ends else 0)
+
+    def chunk_mean(c):
+        return tuple(means[0, kind, mean_rows(c), :] for kind in range(2))
 
     def add(k, at, value, keep=None):
         if keep is not None:
             value = jnp.where(keep, value, 0.0)
         totals[k, pl.ds(at, 8), :] += value
 
-    wrapped = ((rows - CH + REACH, sub < CH - REACH), (REACH - CH, sub >= CH - REACH))
-
-    def own_group(c):
-        lag_group(1, c * CH + REACH)
-        for k in range(25):
-            add(k, 8 + c * CH + REACH, lag_plane(k))
-
-    def own_wrap():
-        lag_group(1, rows - CH + REACH)
+    def own_group(row_at, parts):
+        lag_group(1, row_at)
         for k in range(25):
             plane = lag_plane(k)
-            for start, keep in wrapped:
+            for start, keep in parts:
                 add(k, 8 + start, plane, keep)
 
-    def add_far(at, base, keep=None):
+    def add_far(m, base, keep, ends):
+        at = 16 * m
         gap = {}
         for a in range(-REACH, REACH + 1):
             value, edge = (
@@ -357,45 +379,38 @@
             for b in range(-REACH, REACH + 1):
                 gap[a, b] = shifted(value, edge, b)
         centre = gap[0, 0] * 0.25
-        side = got[at, 13]
+        side = got[at + 13]
         for k in range(25):
             a, b = k // 5 - REACH, k % 5 - REACH
             value = centre * gap[a, b]
             if k >= 12:
-                plane = got[at, k - 12]
+                plane = got[at + k - 12]
                 value = value + plane
                 if k > 12:
                     moved = pltpu.roll(plane, b % LANES, 1)
                     inside = (lane >= b) & (lane < LANES + b)
                     add(24 - k, base + a, jnp.where(inside, moved, 0.0), keep)
             else:
+                direct = None
+                if ends and a < 0:
+                    direct = sub == 6 if a == -1 else sub >= 6
                 if b != 0:
-                    column = pltpu.roll(side, (2 * LANES - 4 * k - 2) % LANES, 1)
                     outside = (lane < -b) | (lane >= LANES - b)
-                    if keep is not None:
-                        outside = outside & (sub != 6 if a == -1 else sub < 6) if a < 0 else outside
-                    value = value + jnp.where(outside, column, 0.0)
-                if keep is not None and a < 0:
-                    direct = sub == 6 if a == -1 else sub >= 6
-                    value = value + jnp.where(direct, got[at + 1, k], 0.0)
+                    if direct is not None:
+                        outside = outside & jnp.logical_not(direct)
+                    value = value + jnp.where(outside, unput(side, k), 0.0)
+                if direct is not None:
+                    low = pltpu.roll(got[at + 15 + k // 4], 6 - 2 * (k % 4), 0)
+                    value = value + jnp.where(direct, low, 0.0)
             add(k, base, value, keep)
 
-    def take_group(at, c):
-        to_partner(at, 1).wait_recv()
-        for kind in range(2):
-            far_means[kind, mean_rows(c), :] = got[at, 14 + kind]
-        add_far(at, 8 + c * CH + REACH)
-
-    def take_wrap():
-        to_partner(WRAP, 2).wait_recv()
-        for kind in range(2):
-            far_means[kind, mean_rows(0), :] = got[WRAP, 14 + kind]
-            far_means[kind, mean_rows(chunks - 1), :] = got[WRAP + 1, 12 + kind]
-            ends = got[WRAP + 1, 14 + kind]
-            far_means[kind, pl.ds(0, 8), :] = jnp.where(sub >= 8 - REACH, ends, 0.0)
-            far_means[kind, pl.ds(8 + rows, 8), :] = jnp.where(sub < REACH, ends, 0.0)
-        for start, keep in wrapped:
-            add_far(WRAP, 8 + start, keep)
+    def take_means(m, n, where):
+        far_means[0, where, :] = got[16 * m + 14 + n]
+        far_means[1, where, :] = unput(got[16 * m + 13], 12 + n)
+
+    def take_group(m, parts, ends=False):
+        for start, keep in parts:
+            add_far(m, 8 + start, keep, ends)
 
     take_chunk(0)
     give_rows(0, 0, 0)
@@ -410,13 +425,16 @@
     @pl.when(has_below)
     def _():
         row_copy(1, below).start()
+
+    send_group(0, inner_ends()[0], (chunk_mean(chunks - 1), chunk_mean(0)))
+    own_group(*inner_ends())
 
     @pl.loop(2, chunks - 1)
     def _(step):
         c = chunk_at(step)
         take_chunk(step)
 
-        @pl.when(step == 3)
+        @pl.when(step == 4)
         def _():
             empty = jnp.zeros((2, REACH, n_half, 5, 8, LANES), F32)
 
@@ -438,34 +456,43 @@
             def _():
                 spread[:, 0:REACH] = empty
 
-            send_wrap()
-
-        send_group(step, c)
-        own_group(c)
-
-        @pl.when(step == 3)
-        def _():
-            own_wrap()
+        send_group(step - 1, plain(c)[0], (chunk_mean(c),))
+        own_group(*plain(c))
 
     last = chunks - 1
     take_chunk(last)
-    send_group(last, 1)
-    send_group(last + 1, 0)
-    own_group(1)
-    own_group(0)
-    take_wrap()
-
-    @pl.loop(2, last)
+    send_group(last - 1, plain(1)[0], (chunk_mean(1),))
+    beyond = tuple(
+        means[0, kind, pl.ds(0, 8), :] + means[0, kind, pl.ds(8 + rows, 8), :] for kind in range(2)
+    )
+    send_group(last, outer_ends()[0], (beyond,), ends=True)
+    own_group(*plain(1))
+    own_group(*outer_ends())
+
+    to_partner(0, planes(2)).wait_recv()
+    take_means(0, 0, mean_rows(chunks - 1))
+    take_means(0, 1, mean_rows(0))
+    take_group(0, inner_ends()[1])
+
+    @pl.loop(2, chunks)
     def _(step):
-        take_group(step, chunk_at(step))
-
-    take_group(last, 1)
-    take_group(last + 1, 0)
+        c = chunk_at(step)
+        to_partner(step - 1, planes(1)).wait_recv()
+        take_means(step - 1, 0, mean_rows(c))
+        take_group(step - 1, plain(c)[1])
+
+    to_partner(last, planes(1, True)).wait_recv()
+    ends = (got[16 * last + 14], unput(got[16 * last + 13], 12))
+    for kind in range(2):
+        far_means[kind, pl.ds(0, 8), :] = jnp.where(sub >= 8 - REACH, ends[kind], 0.0)
+        far_means[kind, pl.ds(8 + rows, 8), :] = jnp.where(sub < REACH, ends[kind], 0.0)
+    take_group(last, outer_ends()[1], ends=True)
     out[...] = totals[:, 8 : 8 + rows, :]
 
     all_of(block.at[:, :, pl.ds(0, n_half - 1)], send_sem, recv_sem.at[0]).wait_send()
     all_of(edges_in.at[:, pl.ds(0, n_half - 1)], edge_send, edge_recv).wait_send()
-    to_partner(0, chunks + 1).wait_send()
+    every = sent.at[pl.ds(0, planes(2) + (chunks - 2) * planes(1) + planes(1, True))]
+    all_of(every, part_send, part_recv.at[0]).wait_send()
 
     @pl.when(has_above)
     def _():
@@ -499,13 +526,13 @@
             pltpu.VMEM((frames * rows, LANES), F32),
             pltpu.VMEM((n_frame * CH * 8, LANES), F32),
             pltpu.VMEM((25, CH * 8, LANES), F32),
-            pltpu.VMEM((chunks + 1, 16, 8, LANES), F32),
-            pltpu.VMEM((chunks + 1, 16, 8, LANES), F32),
+            pltpu.VMEM((16 * chunks + 2, 8, LANES), F32),
+            pltpu.VMEM((16 * chunks + 2, 8, LANES), F32),
             pltpu.VMEM((2, 2, padded, LANES), F32),
             pltpu.VMEM((2, padded, LANES), F32),
             pltpu.VMEM((25, padded, LANES), F32),
             DMA, DMA((chunks,)), DMA, DMA, DMA, DMA, DMA((2,)), DMA((2,)),
-            DMA, DMA((chunks + 1,)),
+            DMA, DMA((chunks,)),
         ],
         compiler_params=pltpu.CompilerParams(
             collective_id=0, has_side_effects=True, vmem_limit_bytes=56 * 2**20

time: 56.3 us -> 54.2 us (0.963)
  the two profiles are of different devices: /device:TPU:24 before, /device:TPU:57 now
where the time goes in v6:
time: 54.2 us; the launch traced here: 54 us
  Pallas kernels  51.9 us (96%)
  local copies, waits for them, and re-layouts  2.12 us (4%)
    pallas_call x1, Pallas kernels, body(): pl.pallas_call(kernel, out_shape=jax.ShapeDtypeStruct((25, rows, width //...  51.9 us
    unnamed x1, local copies, waits for them, and re-layouts  2.12 us

profile of v6, /device:TPU:57, one launch (start us, length us, event | category | flops | bytes accessed | tf_op | source)
XLA Modules:
  0.0 54.0 jit_solution(14790643905194091274)
XLA Ops:
  0.0 51.9 %lag_maps.1 = f32[25,64,128]{2,1,0:T(8,128)} custom-call(bf16[8,64,2048]{2,1,0:T(8,128)(2,1)} %movie.1), custom_call_target="tpu_custom_call" | custom-call | tf_op jit(solution)/shard_map/lag_maps/pallas_call | solution.py:513
  51.9 2.1 %copy.3 = f32[25,64,128]{2,1,0:T(8,128)} copy(f32[25,64,128]{2,1,0:T(8,128)} %lag_maps.1) | data formatting | bytes 1638400

commit v7 on v6

--- a/solution.py
+++ b/solution.py
@@ -85,15 +85,15 @@
     above, below = jnp.maximum(strip - 1, 0), jnp.minimum(strip + 1, n_strip - 1)
     has_above, has_below = strip > 0, strip < n_strip - 1
 
-    whole = pltpu.make_async_copy(movie, held, held_sem)
-    whole.start()
-
-    @pl.loop(0, chunks)
-    def _(c):
-        own_copy(c, 0).start()
-        own_copy(c, 1).start()
-
     barrier = pltpu.get_barrier_semaphore()
+
+    @pl.when(has_above)
+    def _():
+        pl.semaphore_signal(barrier, inc=1, device_id={"strip": above}, device_id_type=MESH)
+
+    @pl.when(has_below)
+    def _():
+        pl.semaphore_signal(barrier, inc=1, device_id={"strip": below}, device_id_type=MESH)
 
     @pl.loop(1, n_half)
     def _(k):
@@ -103,13 +103,13 @@
 
     pl.semaphore_signal(barrier, inc=1, device_id={"frame": partner}, device_id_type=MESH)
 
-    @pl.when(has_above)
-    def _():
-        pl.semaphore_signal(barrier, inc=1, device_id={"strip": above}, device_id_type=MESH)
-
-    @pl.when(has_below)
-    def _():
-        pl.semaphore_signal(barrier, inc=1, device_id={"strip": below}, device_id_type=MESH)
+    whole = pltpu.make_async_copy(movie, held, held_sem)
+    whole.start()
+
+    @pl.loop(0, chunks)
+    def _(c):
+        own_copy(c, 0).start()
+        own_copy(c, 1).start()
 
     totals[...] = jnp.zeros(totals.shape, F32)
     means[...] = jnp.zeros(means.shape, F32)
@@ -224,23 +224,22 @@
         def _():
             all_of(edges_in.at[:, pl.ds(0, n_half - 1)], edge_send, edge_recv).wait_recv()
 
-        edge_totals = []
-        for slot in range(2):
-            edge_total = edge_tile(slot, 0, c)
-            for i in range(1, n_half):
-                edge_total = edge_total + edge_tile(slot, i, c)
-            edge_totals.append(edge_total)
-
-        @pl.loop(0, CH, unroll=2)
+        prepare_chunk(0, c)
+
+    def prepare_chunk(slot, c):
+        edge_total = edge_tile(slot, 0, c)
+        for i in range(1, n_half):
+            edge_total = edge_total + edge_tile(slot, i, c)
+
+        @pl.loop(0, CH, unroll=4)
         def _(r):
             turn = edge_turn(c, r)
-            for slot in range(2):
-                prepare(
-                    slot, c * CH + r,
-                    lambda i: work_row(slot, i, r),
-                    lambda i: pltpu.roll(edge_tile(slot, i, c), turn, 1),
-                    pltpu.roll(edge_totals[slot], turn, 1),
-                )
+            prepare(
+                slot, c * CH + r,
+                lambda i: work_row(slot, i, r),
+                lambda i: pltpu.roll(edge_tile(slot, i, c), turn, 1),
+                pltpu.roll(edge_total, turn, 1),
+            )
 
     def place(slot, r, i):
         return (slot * REACH + r) * n_half + i
@@ -276,8 +275,8 @@
                     edge_of, edge_total,
                 )
 
-    def lag_group(slot, row_at):
-        @pl.loop(0, CH)
+    def lag_group(slot, row_at, count):
+        @pl.loop(0, count)
         def _(n):
             r = row_at(n)
             sums = [None] * 25
@@ -316,19 +315,30 @@
 
     def outer_ends():
         return (
-            lambda n: jnp.where(n < 4, CH - REACH + n, lax.rem(rows - CH + REACH + n, rows)),
-            (
-                (CH - REACH, sub < 4),
-                (rows - CH + REACH, (sub >= 4) & (sub < 6)),
-                (REACH - CH, sub >= 6),
-            ),
+            lambda n: lax.rem(rows - REACH + n, rows),
+            ((rows - REACH, sub < 2), (-REACH, (sub >= 2) & (sub < 4))),
         )
 
-    def send_group(m, row_at, chunk_means, ends=False):
+    def last_rows():
+        return (lambda n: CH - REACH + n), ((CH - REACH, sub < 4),)
+
+    def layout(count, n_means, ends):
+        side = 13 if count == CH else 7
+        return side, side + 1, side + 1 + n_means, side + 1 + n_means + (3 if ends else 0)
+
+    def send_group(m, row_at, chunk_means, count=CH, ends=False):
         at = 16 * m
-        lag_group(0, row_at)
-        for p in range(13):
-            sent[at + p] = lag_plane(12 + p)
+        side_at, mean_at, low_at, length = layout(count, len(chunk_means), ends)
+        lag_group(0, row_at, count)
+        if count == CH:
+            for p in range(13):
+                sent[at + p] = lag_plane(12 + p)
+        else:
+            for p in range(0, 13, 2):
+                pair = lag_plane(12 + p)
+                if p < 12:
+                    pair = jnp.where(sub < 4, pair, pltpu.roll(lag_plane(13 + p), 4, 0))
+                sent[at + p // 2] = pair
         side, low = zero, [zero] * 3
         for k in range(12):
             if k % 5 == REACH and not ends:
@@ -337,21 +347,18 @@
             if k % 5 != REACH:
                 side = jnp.where(group == k, put(plane, k), side)
             if ends:
-                place = 2 * (k % 4)
+                turn = (2 * (k % 4) - 2) % 8
                 low[k // 4] = jnp.where(
-                    sub // 2 == k % 4, pltpu.roll(plane, (place + 2) % 8, 0), low[k // 4]
+                    sub // 2 == k % 4, pltpu.roll(plane, turn, 0), low[k // 4]
                 )
         for n, (mean, edge) in enumerate(chunk_means):
-            sent[at + 14 + n] = mean
+            sent[at + mean_at + n] = mean
             side = jnp.where(group == 12 + n, put(edge, 12 + n), side)
-        sent[at + 13] = side
+        sent[at + side_at] = side
         if ends:
             for n in range(3):
-                sent[at + 15 + n] = low[n]
-        to_partner(m, planes(len(chunk_means), ends)).start()
-
-    def planes(n_means, ends=False):
-        return 14 + n_means + (3 if ends else 0)
+                sent[at + low_at + n] = low[n]
+        to_partner(m, length).start()
 
     def chunk_mean(c):
         return tuple(means[0, kind, mean_rows(c), :] for kind in range(2))
@@ -361,15 +368,16 @@
             value = jnp.where(keep, value, 0.0)
         totals[k, pl.ds(at, 8), :] += value
 
-    def own_group(row_at, parts):
-        lag_group(1, row_at)
+    def own_group(row_at, parts, count=CH):
+        lag_group(1, row_at, count)
         for k in range(25):
             plane = lag_plane(k)
             for start, keep in parts:
                 add(k, 8 + start, plane, keep)
 
-    def add_far(m, base, keep, ends):
+    def add_far(m, base, keep, count, n_means, ends):
         at = 16 * m
+        side_at, _, low_at, _ = layout(count, n_means, ends)
         gap = {}
         for a in range(-REACH, REACH + 1):
             value, edge = (
@@ -379,12 +387,18 @@
             for b in range(-REACH, REACH + 1):
                 gap[a, b] = shifted(value, edge, b)
         centre = gap[0, 0] * 0.25
-        side = got[at + 13]
+        side = got[at + side_at]
         for k in range(25):
             a, b = k // 5 - REACH, k % 5 - REACH
             value = centre * gap[a, b]
             if k >= 12:
-                plane = got[at + k - 12]
+                p = k - 12
+                if count == CH:
+                    plane = got[at + p]
+                else:
+                    plane = got[at + p // 2]
+                    if p % 2:
+                        plane = pltpu.roll(plane, 4, 0)
                 value = value + plane
                 if k > 12:
                     moved = pltpu.roll(plane, b % LANES, 1)
@@ -393,14 +407,14 @@
             else:
                 direct = None
                 if ends and a < 0:
-                    direct = sub == 6 if a == -1 else sub >= 6
+                    direct = sub == 2 if a == -1 else (sub == 2) | (sub == 3)
                 if b != 0:
                     outside = (lane < -b) | (lane >= LANES - b)
                     if direct is not None:
                         outside = outside & jnp.logical_not(direct)
                     value = value + jnp.where(outside, unput(side, k), 0.0)
                 if direct is not None:
-                    low = pltpu.roll(got[at + 15 + k // 4], 6 - 2 * (k % 4), 0)
+                    low = pltpu.roll(got[at + low_at + k // 4], (2 - 2 * (k % 4)) % 8, 0)
                     value = value + jnp.where(direct, low, 0.0)
             add(k, base, value, keep)
 
@@ -408,11 +422,15 @@
         far_means[0, where, :] = got[16 * m + 14 + n]
         far_means[1, where, :] = unput(got[16 * m + 13], 12 + n)
 
-    def take_group(m, parts, ends=False):
+    def take_group(m, parts, count=CH, n_means=1, ends=False):
         for start, keep in parts:
-            add_far(m, 8 + start, keep, ends)
+            add_far(m, 8 + start, keep, count, n_means, ends)
+
+    def arrived(m, count, n_means, ends=False):
+        to_partner(m, layout(count, n_means, ends)[3]).wait_recv()
 
     take_chunk(0)
+    prepare_chunk(1, 0)
     give_rows(0, 0, 0)
 
     @pl.when(has_above)
@@ -427,12 +445,19 @@
         row_copy(1, below).start()
 
     send_group(0, inner_ends()[0], (chunk_mean(chunks - 1), chunk_mean(0)))
+    prepare_chunk(1, chunks - 1)
     own_group(*inner_ends())
 
-    @pl.loop(2, chunks - 1)
+    last = chunks - 1
+    wrap = last - 1
+
+    @pl.loop(2, last)
     def _(step):
         c = chunk_at(step)
         take_chunk(step)
+        send_group(step - 1, plain(c)[0], (chunk_mean(c),))
+        prepare_chunk(1, c)
+        own_group(*plain(c))
 
         @pl.when(step == 4)
         def _():
@@ -456,42 +481,57 @@
             def _():
                 spread[:, 0:REACH] = empty
 
-        send_group(step - 1, plain(c)[0], (chunk_mean(c),))
-        own_group(*plain(c))
-
-    last = chunks - 1
-    take_chunk(last)
-    send_group(last - 1, plain(1)[0], (chunk_mean(1),))
-    beyond = tuple(
-        means[0, kind, pl.ds(0, 8), :] + means[0, kind, pl.ds(8 + rows, 8), :] for kind in range(2)
-    )
-    send_group(last, outer_ends()[0], (beyond,), ends=True)
-    own_group(*plain(1))
-    own_group(*outer_ends())
-
-    to_partner(0, planes(2)).wait_recv()
+            beyond = tuple(
+                means[0, kind, pl.ds(0, 8), :] + means[0, kind, pl.ds(8 + rows, 8), :]
+                for kind in range(2)
+            )
+            send_group(wrap, outer_ends()[0], (beyond,), count=4, ends=True)
+            own_group(*outer_ends(), count=4)
+
+    arrived(0, CH, 2)
     take_means(0, 0, mean_rows(chunks - 1))
     take_means(0, 1, mean_rows(0))
-    take_group(0, inner_ends()[1])
-
-    @pl.loop(2, chunks)
-    def _(step):
+    take_group(0, inner_ends()[1], n_means=2)
+
+    def take_step(step):
         c = chunk_at(step)
-        to_partner(step - 1, planes(1)).wait_recv()
+        arrived(step - 1, CH, 1)
         take_means(step - 1, 0, mean_rows(c))
         take_group(step - 1, plain(c)[1])
 
-    to_partner(last, planes(1, True)).wait_recv()
-    ends = (got[16 * last + 14], unput(got[16 * last + 13], 12))
+    @pl.loop(2, last - 1)
+    def _(step):
+        take_step(step)
+
+    arrived(wrap, 4, 1, True)
+    beyond = (got[16 * wrap + 8], unput(got[16 * wrap + 7], 12))
     for kind in range(2):
-        far_means[kind, pl.ds(0, 8), :] = jnp.where(sub >= 8 - REACH, ends[kind], 0.0)
-        far_means[kind, pl.ds(8 + rows, 8), :] = jnp.where(sub < REACH, ends[kind], 0.0)
-    take_group(last, outer_ends()[1], ends=True)
+        far_means[kind, pl.ds(0, 8), :] = jnp.where(sub >= 8 - REACH, beyond[kind], 0.0)
+        far_means[kind, pl.ds(8 + rows, 8), :] = jnp.where(sub < REACH, beyond[kind], 0.0)
+    take_group(wrap, outer_ends()[1], count=4, ends=True)
+
+    take_chunk(last)
+    send_group(last, plain(1)[0], (chunk_mean(1),))
+    send_group(last + 1, last_rows()[0], (), count=4)
+    prepare_chunk(1, 1)
+    own_group(*plain(1))
+    own_group(*last_rows(), count=4)
+
+    take_step(last - 1)
+    arrived(last, CH, 1)
+    take_means(last, 0, mean_rows(1))
+    take_group(last, plain(1)[1])
+    arrived(last + 1, 4, 0)
+    take_group(last + 1, last_rows()[1], count=4, n_means=0)
     out[...] = totals[:, 8 : 8 + rows, :]
 
     all_of(block.at[:, :, pl.ds(0, n_half - 1)], send_sem, recv_sem.at[0]).wait_send()
     all_of(edges_in.at[:, pl.ds(0, n_half - 1)], edge_send, edge_recv).wait_send()
-    every = sent.at[pl.ds(0, planes(2) + (chunks - 2) * planes(1) + planes(1, True))]
+    length = (
+        layout(CH, 2, False)[3] + (chunks - 2) * layout(CH, 1, False)[3]
+        + layout(4, 1, True)[3] + layout(4, 0, False)[3]
+    )
+    every = sent.at[pl.ds(0, length)]
     all_of(every, part_send, part_recv.at[0]).wait_send()
 
     @pl.when(has_above)
@@ -526,13 +566,13 @@
             pltpu.VMEM((frames * rows, LANES), F32),
             pltpu.VMEM((n_frame * CH * 8, LANES), F32),
             pltpu.VMEM((25, CH * 8, LANES), F32),
-            pltpu.VMEM((16 * chunks + 2, 8, LANES), F32),
-            pltpu.VMEM((16 * chunks + 2, 8, LANES), F32),
+            pltpu.VMEM((16 * chunks + 16, 8, LANES), F32),
+            pltpu.VMEM((16 * chunks + 16, 8, LANES), F32),
             pltpu.VMEM((2, 2, padded, LANES), F32),
             pltpu.VMEM((2, padded, LANES), F32),
             pltpu.VMEM((25, padded, LANES), F32),
             DMA, DMA((chunks,)), DMA, DMA, DMA, DMA, DMA((2,)), DMA((2,)),
-            DMA, DMA((chunks,)),
+            DMA, DMA((chunks + 1,)),
         ],
         compiler_params=pltpu.CompilerParams(
             collective_id=0, has_side_effects=True, vmem_limit_bytes=56 * 2**20

time: 54.2 us -> 53.5 us (0.987)
  the two profiles are of different devices: /device:TPU:57 before, /device:TPU:192 now
where the time goes in v7:
time: 53.5 us; the launch traced here: 53.4 us
  Pallas kernels  51.2 us (96%)
  local copies, waits for them, and re-layouts  2.12 us (4%)
    pallas_call x1, Pallas kernels, body(): pl.pallas_call(kernel, out_shape=jax.ShapeDtypeStruct((25, rows, width //...  51.2 us
    unnamed x1, local copies, waits for them, and re-layouts  2.12 us

profile of v7, /device:TPU:192, one launch (start us, length us, event | category | flops | bytes accessed | tf_op | source)
XLA Modules:
  0.0 53.4 jit_solution(14812090858423287134)
XLA Ops:
  0.0 51.2 %lag_maps.1 = f32[25,64,128]{2,1,0:T(8,128)} custom-call(bf16[8,64,2048]{2,1,0:T(8,128)(2,1)} %movie.1), custom_call_target="tpu_custom_call" | custom-call | tf_op jit(solution)/shard_map/lag_maps/pallas_call | solution.py:553
  51.3 2.1 %copy.3 = f32[25,64,128]{2,1,0:T(8,128)} copy(f32[25,64,128]{2,1,0:T(8,128)} %lag_maps.1) | data formatting | bytes 1638400
